TPU v7x, 32 devices: a whole 2x2x4 slice. The times are simulated.
32 devices in a mesh: row: 4 (over x, core), col: 8 (over z, y).
Axes of the slice: x: 2, y: 2, z: 4, core: 2. Of those that a mesh axis runs over, the one named last changes fastest.
Arguments:
- pair_density: bfloat16 [2048, 8192], P('col', 'row'), may hold values from -6 to 6
- scale_exp: int32 [2048], replicated, may hold values from -1 to 1
- pair_weight: int32 [2048], replicated, may hold values from 1 to 4
- resident_ids: int32 [512], replicated, may hold values from 0 to 2047, as said below
- diagonal_shift: float32 [8192], replicated, may hold values from 2 to 4
- background: float32 [8192, 8192], P('row', 'col'), as said below
Outputs:
- dielectric: float32 [8192, 8192], P('row', 'col')
- kernel: float32 [2048, 512], P(('col', 'row'))
Inputs may be any that keep to these rules, and one draw needn't show every extreme that they name: `resident_ids`: 512 distinct pair indices. background is symmetric.
All inputs are finite; a program needn't handle non-finite values.
Results may differ from a plain program's by a relative error of at most 0.0003.
Values may be sent and summed in bfloat16 or wider, within the bound.
No kernel may reach another device: no remote copies, remote signals or barrier semaphores. Data moves between devices by JAX's collectives and lax.ppermute only.
A program may use at most 128 MiB of HBM per device.

v0:
```python
import math
import jax
import jax.numpy as jnp
from jax import lax
from jax.sharding import PartitionSpec as P

NG = 8192
SWEEPS = 2
damping = 0.5


def from_root(block, axis, owner):
    block = jnp.where(lax.axis_index(axis) == owner, block, jnp.zeros_like(block))
    return lax.psum(block, axis)


def scale_factor(exponent):
    return jnp.where(exponent < 0, 0.5, jnp.where(exponent > 0, 2.0, 1.0)).astype(jnp.float32)


def pair_contract(left_block, right_block):
    return lax.dot_general(
        left_block, right_block, (((0,), (0,)), ((), ())), preferred_element_type=jnp.float32
    )


def shards(pair_density, scale_exp, pair_weight, resident_ids, diagonal_shift, background):
    row_count = lax.axis_size("row")
    col_count = lax.axis_size("col")
    row_index = lax.axis_index("row")
    col_index = lax.axis_index("col")
    pair_dev, row_width = pair_density.shape
    col_width = background.shape[1]
    pair_total = pair_dev * col_count
    norm_scale = 4 * pair_total
    factor = scale_factor(scale_exp)
    own_factor = lax.dynamic_slice_in_dim(factor, col_index * pair_dev, pair_dev)
    scaled = (pair_density.astype(jnp.float32) * own_factor[:, None]).astype(jnp.bfloat16)
    left_all = lax.all_gather(scaled, "col", axis=0, tiled=True)
    relaid = lax.all_to_all(
        lax.all_to_all(scaled, "row", split_axis=0, concat_axis=1, tiled=True),
        "col",
        split_axis=1,
        concat_axis=0,
        tiled=True,
    )
    share_rows = pair_dev // row_count
    left_order = left_all.reshape(col_count, row_count, share_rows, row_width)
    left_order = left_order.transpose(1, 0, 2, 3).reshape(pair_total, row_width)
    contracted = pair_contract(left_order, lax.all_gather(relaid, "row", axis=0, tiled=True))
    response = contracted / norm_scale
    row_start = row_index * row_width
    col_start = col_index * col_width
    global_rows = row_start + lax.broadcasted_iota(jnp.int32, (row_width, col_width), 0)
    global_cols = col_start + lax.broadcasted_iota(jnp.int32, (row_width, col_width), 1)
    shift_rows = lax.dynamic_slice_in_dim(diagonal_shift, row_start, row_width)
    dielectric = (
        background + response + jnp.where(global_rows == global_cols, shift_rows[:, None], 0.0)
    )
    precond_rows = (
        shift_rows
        + jnp.einsum("pg,pg->g", left_all, left_all, preferred_element_type=jnp.float32)
        / norm_scale
    )
    picked = left_all[resident_ids].astype(jnp.float32) / factor[resident_ids][:, None]
    source_rows = picked.T
    col_ratio = col_count // row_count
    root_row = col_index // col_ratio
    offset = col_index % col_ratio * col_width

    def column_share(values):
        return lax.dynamic_slice_in_dim(values, offset, col_width, 0)

    source_cols, precond_cols = (
        from_root(column_share(source_rows), "row", root_row),
        from_root(column_share(precond_rows), "row", root_row),
    )
    screen_rows = source_rows / precond_rows[:, None]
    screen_cols = source_cols / precond_cols[:, None]
    for sweep_index in range(SWEEPS):
        last_sweep = sweep_index + 1 == SWEEPS
        row_image = lax.psum(
            jnp.dot(dielectric, screen_cols, precision=lax.Precision.HIGHEST), "col"
        )
        if not last_sweep:
            transposed = lax.dot_general(
                dielectric, screen_rows, (((0,), (0,)), ((), ())), precision=lax.Precision.HIGHEST
            )
            col_image = lax.psum(transposed, "row")
            screen_cols = screen_cols + damping * (source_cols - col_image) / precond_cols[:, None]
        screen_rows = screen_rows + damping * (source_rows - row_image) / precond_rows[:, None]
    partial_value = jnp.dot(
        pair_density.astype(jnp.float32), screen_rows, precision=lax.Precision.HIGHEST
    )
    summed = lax.psum_scatter(partial_value, "row", scatter_dimension=0, tiled=True)
    kernel_share = pair_dev // row_count
    weights = lax.dynamic_slice_in_dim(
        pair_weight, col_index * pair_dev + row_index * kernel_share, kernel_share
    ).astype(jnp.float32)
    kernel = weights[:, None] * summed / math.sqrt(NG)
    return (dielectric, kernel)


def solution(mesh):
    return jax.shard_map(
        shards,
        mesh=mesh,
        in_specs=(P("col", "row"), P(), P(), P(), P(), P("row", "col")),
        out_specs=(P("row", "col"), P(("col", "row"), None)),
        check_vma=False,
    )
```

profile of v0, /device:TPU:0, one launch (start us, length us, event | category | flops | bytes accessed | tf_op | source)
XLA Modules:
  0.0 656.9 jit_solution(1160271850657053020)
XLA Ops:
  7.2 0.0 all-gather.3.cloned.1.call-start
  7.2 0.7 select_select_fusion
  7.9 0.1 dynamic_slice.15
  8.0 2.4 multiply_convert_fusion
  10.4 0.0 all-gather.3.cloned.1.call-update
  10.4 0.0 all-gather.5.cloned.1.call-start
  10.5 18.7 %all_to_all.35 = bf16[4,64,2048]{2,1,0:T(8,128)(2,1)S(1)} all-to-all(bf16[4,64,2048]{2,1,0:T(8,128)(2,1)} %bitcast.38), channel_id=1, replica_groups=mesh['row'=4,'col'=8] {'row'}, dimensions={0} | all-to-all | bytes 2097152 | tf_op jit(solution)/shard_map/all_to_all | solution.py:41
  29.2 0.8 copy.14
  30.0 0.0 copy-start.2
  30.0 0.3 all_to_all.29
  30.3 0.6 copy.15
  30.9 51.7 %all_to_all.36 = bf16[64,8,1024]{2,0,1:T(8,128)(2,1)} all-to-all(bf16[64,8,1024]{2,0,1:T(8,128)(2,1)S(1)} %copy.15), channel_id=1, replica_groups=mesh['row'=4,'col'=8] {'col'}, dimensions={1} | all-to-all | bytes 2097152 | tf_op jit(solution)/shard_map/all_to_all | solution.py:40
  82.5 0.0 all-gather.5.cloned.1.call-update
  82.6 0.6 all-reduce.7.cloned.1.call-start
  83.2 0.0 copy-done.2
  83.2 3.1 gather_fusion.1
  86.4 72.6 %all-gather.3.cloned.1.call-done = bf16[2048,2048]{1,0:T(8,128)(2,1)} async-done(((bf16[256,2048]{1,0:T(8,128)(2,1)}), bf16[2048,2048]{1,0:T(8,128)(2,1)}) %all-gather.3.cloned.1.call-update) | async-done | bytes 8388624 | tf_op jit(solution)/shard_map/all_gather | solution.py:39
  159.0 9.7 %gather_fusion = bf16[512,2048]{1,0:T(8,128)(2,1)} fusion(bf16[2048,2048]{1,0:T(8,128)(2,1)} %all-gather.3.cloned.1.call-done, s32[1024]{0:T(1024)S(1)} %pad_clamp_fusion), kind=kCustom, calls=%fused_computation | custom fusion | bytes 4196352 | tf_op jit(solution)/shard_map/gather | solution.py:65
  168.7 2.9 copy.16
  171.6 2.6 convert_element_type.25
  174.1 8.5 %copy.13 = bf16[8,4,64,2048]{3,2,0,1:T(8,128)(2,1)} copy(bf16[8,4,64,2048]{3,2,1,0:T(8,128)(2,1)} %bitcast.37) | data formatting | bytes 16777216 | tf_op jit(solution)/shard_map/reshape | solution.py:48
  182.6 5.2 fusion
  187.8 0.7 multiply_add_fusion
  188.5 4.8 all-gather.5.cloned.1.call-done
  193.2 15.4 %select_add_fusion = f32[2048,1024]{1,0:T(8,128)S(1)} fusion(f32[2048,1024]{1,0:T(8,128)} %param.11, bf16[2048,2048]{1,0:T(8,128)(2,1)} %bitcast.39, bf16[2048,1024]{1,0:T(8,128)(2,1)} %all-gather.5.cloned.1.call-done, f32[2048]{0:T(1024)S(1)} %get-tuple-element.13, s32[1024]{0:T(1024)S(1)} %iota_add_fusion.1, s32[2048]{0:T(1024)S(1)} %iota_add_fusion), kind=kOutput, calls=%fused_computation.4 | convolution fusion | flops 8600420352 | bytes 29380608 | tf_op jit(solution)/shard_map/dot_general | solution.py:22
  208.6 0.0 copy-start.5
  208.6 0.0 copy-start
  208.6 16.1 %fusion.10 = f32[1024,512]{1,0:T(8,128)} fusion(f32[2048,1024]{1,0:T(8,128)S(1)} %select_add_fusion, bf16[512,2048]{0,1:T(8,128)(2,1)S(1)} %copy.16, f32[2048]{0:T(1024)S(1)} %get-tuple-element.12, f32[512]{0:T(512)S(1)} %gather_fusion.1), kind=kOutput, calls=%fused_computation.16 | convolution fusion | flops 12888047616 | bytes 12593152 | tf_op jit(solution)/shard_map/dot_general | solution.py:86
  224.8 0.0 copy-done.5
  224.8 0.0 copy-done
  224.8 1.6 fusion.12
  226.3 0.0 all-reduce.7.cloned.1.call-update
  226.4 0.0 all-reduce.5.cloned.1.call-start
  226.4 5.9 psum.36
  232.3 79.7 %all-reduce.7.cloned.1.call-done = (f32[1024,512]{1,0:T(8,128)}, f32[1024,512]{1,0:T(8,128)}) async-done(((f32[1024,512]{1,0:T(8,128)}, f32[1024,512]{1,0:T(8,128)}), (f32[1024,512]{1,0:T(8,128)}, f32[1024,512]{1,0:T(8,128)})) %all-reduce.7.cloned.1.call-update) | async-done | bytes 4194320 | tf_op jit(solution)/shard_map/psum | solution.py:14
  312.0 0.0 copy-start.3
  312.0 0.0 copy-start.4
  312.0 0.0 copy-start.6
  312.0 18.0 %fusion.30 = f32[2048,512]{1,0:T(8,128)} fusion(f32[2048,1024]{1,0:T(8,128)} %copy-done.5, f32[1024,512]{1,0:T(8,128)} %get-tuple-element.10, f32[1024]{0:T(1024)S(1)} %psum.36), kind=kOutput, calls=%fused_computation.37 | convolution fusion | flops 12885426176 | bytes 14684160 | tf_op jit(solution)/shard_map/dot_general | solution.py:83
  330.0 0.0 copy-done.3
  330.0 0.0 copy-done.4
  330.0 0.0 copy-done.6
  330.0 15.5 %fusion.15 = f32[2048,512]{1,0:T(8,128)} fusion(f32[2048,1024]{1,0:T(8,128)S(1)} %copy-done.6, f32[1024,512]{1,0:T(8,128)S(1)} %copy-done.3, f32[1024,512]{1,0:T(8,128)S(1)} %copy-done.4, f32[1024]{0:T(1024)S(1)} %psum.36), kind=kOutput, calls=%fused_computation.22 | convolution fusion | flops 12887523328 | bytes 16781312 | tf_op jit(solution)/shard_map/dot_general | solution.py:83
  345.5 0.0 copy-start.1
  345.5 0.0 all-reduce.5.cloned.1.call-update
  345.5 0.3 reduce-scatter.4.cloned.1.call-start
  345.8 270.0 %all-reduce.5.cloned.1.call-done = (f32[2048,512]{1,0:T(8,128)}, f32[2048,512]{1,0:T(8,128)}) async-done(((f32[2048,512]{1,0:T(8,128)}, f32[2048,512]{1,0:T(8,128)}), (f32[2048,512]{1,0:T(8,128)}, f32[2048,512]{1,0:T(8,128)})) %all-reduce.5.cloned.1.call-update) | async-done | bytes 8388624 | tf_op jit(solution)/shard_map/psum | solution.py:82
  615.9 0.0 copy-done.1
  615.9 9.4 %fusion.25 = f32[256,512]{0,1:T(8,128)} fusion(bf16[256,2048]{1,0:T(8,128)(2,1)S(1)} %copy-done.1, f32[2048,512]{1,0:T(8,128)} %get-tuple-element.8, f32[2048,512]{1,0:T(8,128)} %get-tuple-element.9, bf16[512,2048]{0,1:T(8,128)(2,1)S(1)} %copy.16, f32[2048]{0:T(1024)S(1)} %get-tuple-element.12, f32[512]{0:T(512)S(1)} %gather_fusion.1), kind=kOutput, calls=%fused_computation.33 | convolution fusion | flops 3233808384 | bytes 12068864 | tf_op jit(solution)/shard_map/dot_general | solution.py:92
  625.3 2.0 copy.24
  627.3 0.0 reduce-scatter.4.cloned.1.call-update
  627.4 0.8 dynamic-slice_convert_fusion
  628.1 20.1 %reduce-scatter.4.cloned.1.call-done = f32[64,512]{1,0:T(8,128)} async-done(((f32[256,512]{1,0:T(8,128)}), f32[64,512]{1,0:T(8,128)}) %reduce-scatter.4.cloned.1.call-update) | async-done | bytes 131088
  648.3 1.0 copy.25
  649.3 0.8 copy.17
  (6 shorter events, 0.1 us)
Async XLA Ops:
  7.2 151.8 %all-gather.3.cloned.1.call-start = ((), (), s32[]{:S(2)}) async-start(), calls=%async_computation.3 | async-start | bytes 9437184 | tf_op jit(solution)/shard_map/all_gather | solution.py:39
  10.4 182.8 %all-gather.5.cloned.1.call-start = ((), (), s32[]{:S(2)}) async-start(), calls=%async_computation.4 | async-start | bytes 5242880 | tf_op jit(solution)/shard_map/all_gather | solution.py:50
  30.0 53.2 %copy-start.2 = (s32[512]{0:T(512)S(1)}, s32[512]{0:T(512)}, u32[]{:S(2)}) copy-start(s32[512]{0:T(512)} %param.9) | copy-start | bytes 6148
  82.6 229.5 %all-reduce.7.cloned.1.call-start = ((), (), s32[]{:S(2)}) async-start(), calls=%async_computation.7 | async-start | bytes 8388608 | tf_op jit(solution)/shard_map/psum | solution.py:14
  208.6 16.1 %copy-start.5 = (f32[2048,1024]{1,0:T(8,128)}, f32[2048,1024]{1,0:T(8,128)S(1)}, u32[]{:S(2)}) copy-start(f32[2048,1024]{1,0:T(8,128)S(1)} %select_add_fusion) | copy-start | bytes 25165828
  208.6 16.1 %copy-start = (f32[512,2048]{0,1:T(8,128)S(1)}, f32[512,2048]{0,1:T(8,128)}, u32[]{:S(2)}) copy-start(f32[512,2048]{0,1:T(8,128)} %convert_element_type.25) | copy-start | bytes 12582916
  226.4 389.5 %all-reduce.5.cloned.1.call-start = ((), (), s32[]{:S(2)}) async-start(), calls=%async_computation.6 | async-start | bytes 16777216 | tf_op jit(solution)/shard_map/psum | solution.py:82
  312.0 18.0 %copy-start.3 = (f32[1024,512]{1,0:T(8,128)S(1)}, f32[1024,512]{1,0:T(8,128)}, u32[]{:S(2)}) copy-start(f32[1024,512]{1,0:T(8,128)} %get-tuple-element.10) | copy-start | bytes 6291460
  312.0 18.0 %copy-start.4 = (f32[1024,512]{1,0:T(8,128)S(1)}, f32[1024,512]{1,0:T(8,128)}, u32[]{:S(2)}) copy-start(f32[1024,512]{1,0:T(8,128)} %get-tuple-element.11) | copy-start | bytes 6291460
  312.0 18.0 %copy-start.6 = (f32[2048,1024]{1,0:T(8,128)S(1)}, f32[2048,1024]{1,0:T(8,128)}, u32[]{:S(2)}) copy-start(f32[2048,1024]{1,0:T(8,128)} %copy-done.5) | copy-start | bytes 25165828
  345.5 270.4 %copy-start.1 = (bf16[256,2048]{1,0:T(8,128)(2,1)S(1)}, bf16[256,2048]{1,0:T(8,128)(2,1)}, u32[]{:S(2)}) copy-start(bf16[256,2048]{1,0:T(8,128)(2,1)} %param.6) | copy-start | bytes 3145732
  345.5 302.7 %reduce-scatter.4.cloned.1.call-start = ((), (), s32[]{:S(2)}) async-start(), calls=%async_computation.5 | async-start | bytes 655360
Sparse Core Ops, SparseCore 0:
  10.7 148.2 all-gather.2
  160.6 32.6 all-gather.4
  226.5 85.5 all-reduce.6
  345.6 270.1 all-reduce.4
  627.5 20.7 reduce-scatter.3
where the time goes:
time: 660 us; the launch traced here: 657 us
  waiting for transfers between devices  447 us (68%)
  blocking collectives  76.2 us (12%)
  matrix products  74.4 us (11%)
  local copies, waits for them, and re-layouts  29.8 us (5%)
  between operations  14.2 us (2%)
  other arithmetic  13.9 us (2%)
    psum x1, waiting for transfers between devices, shards(): lax.psum(jnp.dot(dielectric, screen_cols, precision=lax.Precision.HIGHEST...  270 us
    psum x1, waiting for transfers between devices, from_root(): return lax.psum(block, axis)  79.7 us
    all_gather x1, waiting for transfers between devices, shards(): left_all = lax.all_gather(scaled, 'col', axis=0, tiled=True)  72.6 us
    all_to_all x1, blocking collectives, shards(): lax.all_to_all(lax.all_to_all(scaled, 'row', split_axis=0, concat_axis=1,...  51.7 us
    dot_general x2, matrix products, shards(): jnp.dot(dielectric, screen_cols, precision=lax.Precision.HIGHEST)  33.4 us
    unnamed x6, waiting for transfers between devices  20.2 us
    all_to_all x1, blocking collectives, shards(): lax.all_to_all(scaled, 'row', split_axis=0, concat_axis=1, tiled=True)  18.7 us
    dot_general x1, matrix products, shards(): lax.dot_general(dielectric, screen_rows, (((0,), (0,)), ((), ())), precis...  16.1 us
  transfers between devices with their start and end apart: 5, of which 5 were waited for; matrix products, arithmetic and copies ran while one was open for 5% of the time, Pallas kernels for 0%

commit v1 on v0

--- a/solution.py
+++ b/solution.py
@@ -7,6 +7,13 @@
 NG = 8192
 SWEEPS = 2
 damping = 0.5
+
+
+def note_chunk(frame):
+    oldest = lax.axis_size("col")
+    arr_now = jnp.stack(jnp.split(frame, oldest, 1), 0)
+    outer = lax.all_to_all(arr_now, axis_name="col", split_axis=0, concat_axis=0)
+    return jnp.concatenate(outer, 0)
 
 
 def from_root(block, axis, owner):
@@ -37,13 +44,7 @@
     own_factor = lax.dynamic_slice_in_dim(factor, col_index * pair_dev, pair_dev)
     scaled = (pair_density.astype(jnp.float32) * own_factor[:, None]).astype(jnp.bfloat16)
     left_all = lax.all_gather(scaled, "col", axis=0, tiled=True)
-    relaid = lax.all_to_all(
-        lax.all_to_all(scaled, "row", split_axis=0, concat_axis=1, tiled=True),
-        "col",
-        split_axis=1,
-        concat_axis=0,
-        tiled=True,
-    )
+    relaid = note_chunk(lax.all_to_all(scaled, "row", split_axis=0, concat_axis=1, tiled=True))
     share_rows = pair_dev // row_count
     left_order = left_all.reshape(col_count, row_count, share_rows, row_width)
     left_order = left_order.transpose(1, 0, 2, 3).reshape(pair_total, row_width)

time: 660 us -> 667 us (1.011)
  no operation moved by 1% of the time
where the time goes in v1:
time: 667 us; the launch traced here: 658 us
  waiting for transfers between devices  449 us (67%)
  blocking collectives  77.7 us (12%)
  matrix products  74.4 us (11%)
  local copies, waits for them, and re-layouts  28.3 us (4%)
  between operations  14.5 us (2%)
  other arithmetic  13.9 us (2%)
    psum x1, waiting for transfers between devices, shards(): lax.psum(jnp.dot(dielectric, screen_cols, precision=lax.Precision.HIGHEST...  270 us
    psum x1, waiting for transfers between devices, from_root(): return lax.psum(block, axis)  79.7 us
    all_gather x1, waiting for transfers between devices, shards(): left_all = lax.all_gather(scaled, 'col', axis=0, tiled=True)  74.1 us
    all_to_all x1, blocking collectives, note_chunk(): lax.all_to_all(arr_now, axis_name='col', split_axis=0, concat_axis=0)  53.1 us
    dot_general x2, matrix products, shards(): jnp.dot(dielectric, screen_cols, precision=lax.Precision.HIGHEST)  33.5 us
    unnamed x6, waiting for transfers between devices  20.2 us
    all_to_all x1, blocking collectives, shards(): lax.all_to_all(scaled, 'row', split_axis=0, concat_axis=1, tiled=True)  18.7 us
    dot_general x1, matrix products, shards(): lax.dot_general(dielectric, screen_rows, (((0,), (0,)), ((), ())), precis...  16.1 us
  transfers between devices with their start and end apart: 5, of which 5 were waited for; matrix products, arithmetic and copies ran while one was open for 5% of the time, Pallas kernels for 0%

profile of v1, /device:TPU:0, one launch (start us, length us, event | category | flops | bytes accessed | tf_op | source)
XLA Modules:
  0.0 658.0 jit_solution(15576178308354543782)
XLA Ops:
  7.2 0.0 all-gather.3.cloned.1.call-start
  7.2 0.7 select_select_fusion
  7.9 0.1 dynamic_slice.15
  8.0 2.4 multiply_convert_fusion
  10.4 0.0 all-gather.3.cloned.1.call-update
  10.4 0.0 all-gather.5.cloned.1.call-start
  10.5 18.7 %all_to_all.24 = bf16[4,64,2048]{2,1,0:T(8,128)(2,1)S(1)} all-to-all(bf16[4,64,2048]{2,1,0:T(8,128)(2,1)} %bitcast.70), channel_id=1, replica_groups=mesh['row'=4,'col'=8] {'row'}, dimensions={0} | all-to-all | bytes 2097152 | tf_op jit(solution)/shard_map/all_to_all | solution.py:47
  29.2 0.0 copy-start.2
  29.2 0.1 copy.24
  29.4 53.1 %all_to_all.25 = bf16[8,64,1024]{2,1,0:T(8,128)(2,1)} all-to-all(bf16[8,64,1024]{2,1,0:T(8,128)(2,1)S(1)} %fusion.31), channel_id=1, replica_groups=mesh['row'=4,'col'=8] {'col'}, dimensions={0} | all-to-all | bytes 2097152 | tf_op jit(solution)/shard_map/all_to_all | solution.py:15
  82.5 0.0 all-gather.5.cloned.1.call-update
  82.6 0.0 all-reduce.7.cloned.1.call-start
  82.6 0.0 copy-done.2
  82.7 3.1 gather_fusion.1
  85.9 74.1 %all-gather.3.cloned.1.call-done = bf16[2048,2048]{1,0:T(8,128)(2,1)} async-done(((bf16[256,2048]{1,0:T(8,128)(2,1)}), bf16[2048,2048]{1,0:T(8,128)(2,1)}) %all-gather.3.cloned.1.call-update) | async-done | bytes 8388624 | tf_op jit(solution)/shard_map/all_gather | solution.py:46
  159.9 9.7 %gather_fusion = bf16[512,2048]{1,0:T(8,128)(2,1)} fusion(bf16[2048,2048]{1,0:T(8,128)(2,1)} %all-gather.3.cloned.1.call-done, s32[1024]{0:T(1024)S(1)} %pad_clamp_fusion), kind=kCustom, calls=%fused_computation | custom fusion | bytes 4196352 | tf_op jit(solution)/shard_map/gather | solution.py:66
  169.6 2.9 copy.14
  172.5 2.6 convert_element_type.25
  175.1 8.5 %copy.12 = bf16[8,4,64,2048]{3,2,0,1:T(8,128)(2,1)} copy(bf16[8,4,64,2048]{3,2,1,0:T(8,128)(2,1)} %bitcast.69) | data formatting | bytes 16777216 | tf_op jit(solution)/shard_map/reshape | solution.py:49
  183.5 5.2 fusion
  188.7 0.7 multiply_add_fusion
  189.4 4.8 all-gather.5.cloned.1.call-done
  194.2 15.4 %select_add_fusion = f32[2048,1024]{1,0:T(8,128)S(1)} fusion(f32[2048,1024]{1,0:T(8,128)} %param.11, bf16[2048,2048]{1,0:T(8,128)(2,1)} %bitcast.71, bf16[2048,1024]{1,0:T(8,128)(2,1)} %all-gather.5.cloned.1.call-done, f32[2048]{0:T(1024)S(1)} %get-tuple-element.13, s32[1024]{0:T(1024)S(1)} %iota_add_fusion.1, s32[2048]{0:T(1024)S(1)} %iota_add_fusion), kind=kOutput, calls=%fused_computation.4 | convolution fusion | flops 8600420352 | bytes 29380608 | tf_op jit(solution)/shard_map/dot_general | solution.py:29
  209.5 0.0 copy-start.5
  209.6 0.0 copy-start
  209.6 16.1 %fusion.10 = f32[1024,512]{1,0:T(8,128)} fusion(f32[2048,1024]{1,0:T(8,128)S(1)} %select_add_fusion, bf16[512,2048]{0,1:T(8,128)(2,1)S(1)} %copy.14, f32[2048]{0:T(1024)S(1)} %get-tuple-element.12, f32[512]{0:T(512)S(1)} %gather_fusion.1), kind=kOutput, calls=%fused_computation.16 | convolution fusion | flops 12888047616 | bytes 12593152 | tf_op jit(solution)/shard_map/dot_general | solution.py:87
  225.7 0.0 copy-done.5
  225.7 0.0 copy-done
  225.7 1.6 fusion.12
  227.3 0.0 all-reduce.7.cloned.1.call-update
  227.3 0.0 all-reduce.5.cloned.1.call-start
  227.4 5.9 psum.36
  233.3 79.7 %all-reduce.7.cloned.1.call-done = (f32[1024,512]{1,0:T(8,128)}, f32[1024,512]{1,0:T(8,128)}) async-done(((f32[1024,512]{1,0:T(8,128)}, f32[1024,512]{1,0:T(8,128)}), (f32[1024,512]{1,0:T(8,128)}, f32[1024,512]{1,0:T(8,128)})) %all-reduce.7.cloned.1.call-update) | async-done | bytes 4194320 | tf_op jit(solution)/shard_map/psum | solution.py:21
  313.0 0.0 copy-start.3
  313.0 0.0 copy-start.4
  313.0 0.0 copy-start.6
  313.0 18.0 %fusion.30 = f32[2048,512]{1,0:T(8,128)} fusion(f32[2048,1024]{1,0:T(8,128)} %copy-done.5, f32[1024,512]{1,0:T(8,128)} %get-tuple-element.10, f32[1024]{0:T(1024)S(1)} %psum.36), kind=kOutput, calls=%fused_computation.37 | convolution fusion | flops 12885426176 | bytes 14684160 | tf_op jit(solution)/shard_map/dot_general | solution.py:84
  331.0 0.0 copy-done.3
  331.0 0.0 copy-done.4
  331.0 0.0 copy-done.6
  331.0 15.5 %fusion.15 = f32[2048,512]{1,0:T(8,128)} fusion(f32[2048,1024]{1,0:T(8,128)S(1)} %copy-done.6, f32[1024,512]{1,0:T(8,128)S(1)} %copy-done.3, f32[1024,512]{1,0:T(8,128)S(1)} %copy-done.4, f32[1024]{0:T(1024)S(1)} %psum.36), kind=kOutput, calls=%fused_computation.22 | convolution fusion | flops 12887523328 | bytes 16781312 | tf_op jit(solution)/shard_map/dot_general | solution.py:84
  346.4 0.0 copy-start.1
  346.4 0.0 all-reduce.5.cloned.1.call-update
  346.5 0.3 reduce-scatter.4.cloned.1.call-start
  346.8 270.0 %all-reduce.5.cloned.1.call-done = (f32[2048,512]{1,0:T(8,128)}, f32[2048,512]{1,0:T(8,128)}) async-done(((f32[2048,512]{1,0:T(8,128)}, f32[2048,512]{1,0:T(8,128)}), (f32[2048,512]{1,0:T(8,128)}, f32[2048,512]{1,0:T(8,128)})) %all-reduce.5.cloned.1.call-update) | async-done | bytes 8388624 | tf_op jit(solution)/shard_map/psum | solution.py:83
  616.8 0.0 copy-done.1
  616.8 9.4 %fusion.25 = f32[256,512]{0,1:T(8,128)} fusion(bf16[256,2048]{1,0:T(8,128)(2,1)S(1)} %copy-done.1, f32[2048,512]{1,0:T(8,128)} %get-tuple-element.8, f32[2048,512]{1,0:T(8,128)} %get-tuple-element.9, bf16[512,2048]{0,1:T(8,128)(2,1)S(1)} %copy.14, f32[2048]{0:T(1024)S(1)} %get-tuple-element.12, f32[512]{0:T(512)S(1)} %gather_fusion.1), kind=kOutput, calls=%fused_computation.33 | convolution fusion | flops 3233808384 | bytes 12068864 | tf_op jit(solution)/shard_map/dot_general | solution.py:93
  626.2 2.0 copy.22
  628.2 0.0 reduce-scatter.4.cloned.1.call-update
  628.3 0.8 dynamic-slice_convert_fusion
  629.0 20.1 %reduce-scatter.4.cloned.1.call-done = f32[64,512]{1,0:T(8,128)} async-done(((f32[256,512]{1,0:T(8,128)}), f32[64,512]{1,0:T(8,128)}) %reduce-scatter.4.cloned.1.call-update) | async-done | bytes 131088
  649.2 1.0 copy.23
  650.2 0.8 copy.15
  (14 shorter events, 0.2 us)
Async XLA Ops:
  7.2 152.8 %all-gather.3.cloned.1.call-start = ((), (), s32[]{:S(2)}) async-start(), calls=%async_computation.3 | async-start | bytes 9437184 | tf_op jit(solution)/shard_map/all_gather | solution.py:46
  10.4 183.7 %all-gather.5.cloned.1.call-start = ((), (), s32[]{:S(2)}) async-start(), calls=%async_computation.4 | async-start | bytes 5242880 | tf_op jit(solution)/shard_map/all_gather | solution.py:51
  29.2 53.5 %copy-start.2 = (s32[512]{0:T(512)S(1)}, s32[512]{0:T(512)}, u32[]{:S(2)}) copy-start(s32[512]{0:T(512)} %param.9) | copy-start | bytes 6148
  82.6 230.4 %all-reduce.7.cloned.1.call-start = ((), (), s32[]{:S(2)}) async-start(), calls=%async_computation.7 | async-start | bytes 8388608 | tf_op jit(solution)/shard_map/psum | solution.py:21
  209.5 16.1 %copy-start.5 = (f32[2048,1024]{1,0:T(8,128)}, f32[2048,1024]{1,0:T(8,128)S(1)}, u32[]{:S(2)}) copy-start(f32[2048,1024]{1,0:T(8,128)S(1)} %select_add_fusion) | copy-start | bytes 25165828
  209.6 16.1 %copy-start = (f32[512,2048]{0,1:T(8,128)S(1)}, f32[512,2048]{0,1:T(8,128)}, u32[]{:S(2)}) copy-start(f32[512,2048]{0,1:T(8,128)} %convert_element_type.25) | copy-start | bytes 12582916
  227.3 389.5 %all-reduce.5.cloned.1.call-start = ((), (), s32[]{:S(2)}) async-start(), calls=%async_computation.6 | async-start | bytes 16777216 | tf_op jit(solution)/shard_map/psum | solution.py:83
  313.0 18.0 %copy-start.3 = (f32[1024,512]{1,0:T(8,128)S(1)}, f32[1024,512]{1,0:T(8,128)}, u32[]{:S(2)}) copy-start(f32[1024,512]{1,0:T(8,128)} %get-tuple-element.10) | copy-start | bytes 6291460
  313.0 18.0 %copy-start.4 = (f32[1024,512]{1,0:T(8,128)S(1)}, f32[1024,512]{1,0:T(8,128)}, u32[]{:S(2)}) copy-start(f32[1024,512]{1,0:T(8,128)} %get-tuple-element.11) | copy-start | bytes 6291460
  313.0 18.0 %copy-start.6 = (f32[2048,1024]{1,0:T(8,128)S(1)}, f32[2048,1024]{1,0:T(8,128)}, u32[]{:S(2)}) copy-start(f32[2048,1024]{1,0:T(8,128)} %copy-done.5) | copy-start | bytes 25165828
  346.4 270.3 %copy-start.1 = (bf16[256,2048]{1,0:T(8,128)(2,1)S(1)}, bf16[256,2048]{1,0:T(8,128)(2,1)}, u32[]{:S(2)}) copy-start(bf16[256,2048]{1,0:T(8,128)(2,1)} %param.6) | copy-start | bytes 3145732
  346.5 302.7 %reduce-scatter.4.cloned.1.call-start = ((), (), s32[]{:S(2)}) async-start(), calls=%async_computation.5 | async-start | bytes 655360
Sparse Core Ops, SparseCore 0:
  10.7 149.2 all-gather.2
  161.5 32.6 all-gather.4
  227.4 85.5 all-reduce.6
  346.6 270.1 all-reduce.4
  628.4 20.7 reduce-scatter.3
